TPU v7x, 512 devices: a whole 4x4x16 slice. The times are simulated.
512 devices in a mesh: lat: 16 (over x, y_lo, core), lon: 32 (over y_hi, z).
Axes of the slice: x: 4, y: 4 (y_hi: 2, y_lo: 2; y = y_hi * 2 + y_lo), z: 16, core: 2. Of those that a mesh axis runs over, the one named last changes fastest.
Arguments:
- tracer: float32 [64, 1440, 864], P('lat', 'lon'), may hold values from 1 to 9
- east_courant: float32 [64, 1440, 32], P('lat', 'lon'), may hold values from -0.3 to 0.3
- north_courant: float32 [64, 1440, 32], P('lat', 'lon'), may hold values from -0.3 to 0.3
- east_limiter: int32 [64, 1440, 32], P('lat', 'lon'), may hold values from 0 to 2
- north_limiter: int32 [64, 1440, 32], P('lat', 'lon'), may hold values from 0 to 2
- filter_keep: int32 [64], P('lat'), may hold values from 1 to 721, as said below
- seed_aerosol: float32 [64, 1440, 32], P('lat', 'lon'), may hold values from 0.5 to 5
- volatility: float32 [27], replicated, may hold values from 0.01 to 1000
- cotangent: float32 [64, 1440, 864], P('lat', 'lon'), may hold values from -6 to 6
Outputs:
- particle: float32 [64, 1440, 864], P('lat', 'lon')
- tracer_adjoint: float32 [64, 1440, 864], P('lat', 'lon')
Inputs may be any that keep to these rules, and one draw needn't show every extreme that they name: `filter_keep`: with d = min(i, 63 - i) for row i: rows with d < 2 keep 1 to 32 wavenumbers, and the rows with d = 1 keep exactly 32; every other row keeps 1440 // 2 + 1.
All inputs are finite; a program needn't handle non-finite values.
Results may differ from a plain program's by a relative error of at most 0.0003.
Values sent between devices are 32-bit elements; how exact they have to be, the bound alone decides.
A program may use at most 128 MiB of HBM per device.

v0:
```python
import math

import jax
import jax.numpy as jnp
from jax import lax
from jax.sharding import PartitionSpec as P

NEWTON = 4
KMAX = 32
POLAR = 2


def with_halo(cells, sides, width, closed):
    for axis, dim in sides:
        count = lax.axis_size(axis)
        ends = count if closed else count - 1
        head = lax.slice_in_dim(cells, 0, width, axis=dim)
        tail = lax.slice_in_dim(cells, cells.shape[dim] - width, cells.shape[dim], axis=dim)
        cells = jnp.concatenate(
            [
                lax.ppermute(tail, axis, [(i, (i + 1) % count) for i in range(ends)]),
                cells,
                lax.ppermute(head, axis, [((i + 1) % count, i) for i in range(ends)]),
            ],
            axis=dim,
        )
    return cells


def spread(values, copies):
    return jnp.repeat(values, copies, axis=-1)


def face_value(far_left, near_left, near_right, far_right, limiter, courant):
    fourth = (7.0 * (near_left + near_right) - (far_left + far_right)) / 12.0
    upwind = jnp.where(courant >= 0.0, near_left, near_right)
    centred = 0.5 * (near_left + near_right)
    return jnp.where(limiter == 0, fourth, jnp.where(limiter == 1, upwind, centred))


def zonal_window(window, courant, limiter, species):
    inner_count = window.shape[1] - 4
    courant_q = spread(courant[:, 2 : inner_count + 3], species)
    limiter_q = spread(limiter[:, 2 : inner_count + 3], species)
    fluxes = courant_q * face_value(
        window[:, 0 : inner_count + 1],
        window[:, 1 : inner_count + 2],
        window[:, 2 : inner_count + 3],
        window[:, 3 : inner_count + 4],
        limiter_q,
        courant_q,
    )
    return window[:, 2 : inner_count + 2] - (fluxes[:, 1:] - fluxes[:, :-1])


def meridional_window(window, courant, limiter, first_row, species):
    inner_count = window.shape[0] - 4
    face_rows = first_row + jnp.arange(inner_count + 1, dtype=jnp.int32)
    opened = jnp.where(face_rows[:, None, None] > 0, courant[2 : inner_count + 3], 0.0)
    courant_q = spread(opened, species)
    limiter_q = spread(limiter[2 : inner_count + 3], species)
    fluxes = courant_q * face_value(
        window[0 : inner_count + 1],
        window[1 : inner_count + 2],
        window[2 : inner_count + 3],
        window[3 : inner_count + 4],
        limiter_q,
        courant_q,
    )
    return window[2 : inner_count + 2] - (fluxes[1:] - fluxes[:-1])


def positive(field):
    return 0.5 * (field + jnp.sqrt(field * field + 1.0))


def level_table(levels, species):
    channel_level = jnp.arange(levels * species, dtype=jnp.int32) // species
    return (channel_level[:, None] == jnp.arange(levels, dtype=jnp.int32)[None, :]).astype(
        jnp.float32
    )


def partition(total_mass, seed_aerosol, volatility):
    levels = seed_aerosol.shape[-1]
    species = volatility.shape[0]
    grouping = level_table(levels, species)
    saturation = jnp.tile(volatility, levels)
    aerosol = seed_aerosol
    for newton_step in range(NEWTON):
        denominator = spread(aerosol, species) + saturation
        fraction = total_mass / denominator
        first_sum = jnp.dot(fraction, grouping, precision=lax.Precision.HIGHEST)
        second_sum = jnp.dot(fraction / denominator, grouping, precision=lax.Precision.HIGHEST)
        residue = 1.0 - seed_aerosol / aerosol - first_sum
        derivative = seed_aerosol / (aerosol * aerosol) + second_sum
        aerosol = aerosol - residue / derivative
    aerosol_q = spread(aerosol, species)
    return total_mass * aerosol_q / (aerosol_q + saturation)


def east_west(field):
    return with_halo(field, (("lon", 1),), 2, True)


def north_south(field):
    return with_halo(field, (("lat", 0),), 2, False)


def fold_rows(gradient):
    inner_rows = gradient.shape[0] - 4
    rim_cells = jnp.concatenate([gradient[:2], gradient[inner_rows + 2 :]], axis=0)
    arrived = north_south(rim_cells)
    middle = gradient[2 : inner_rows + 2]
    return jnp.concatenate(
        [
            middle[:2] + arrived[:2],
            middle[2 : inner_rows - 2],
            middle[inner_rows - 2 :] + arrived[6:],
        ],
        axis=0,
    )


def fold_columns(gradient):
    inner_cols = gradient.shape[1] - 4
    rim_cells = jnp.concatenate([gradient[:, :2], gradient[:, inner_cols + 2 :]], axis=1)
    arrived = east_west(rim_cells)
    middle = gradient[:, 2 : inner_cols + 2]
    return jnp.concatenate(
        [
            middle[:, :2] + arrived[:, :2],
            middle[:, 2 : inner_cols - 2],
            middle[:, inner_cols - 2 :] + arrived[:, 6:],
        ],
        axis=1,
    )


def wave_table(column_count, length):
    position = jnp.arange(column_count, dtype=jnp.int32)
    numbers = jnp.arange(KMAX, dtype=jnp.int32)
    phases = position[:, None] * numbers[None, :] % length
    angles = phases.astype(jnp.float32) * (2.0 * math.pi / length)
    return jnp.concatenate([jnp.cos(angles), jnp.sin(angles)], axis=1)


def wave_weights(keep_values, length):
    numbers = jnp.arange(2 * KMAX, dtype=jnp.int32) % KMAX
    scaling = jnp.where(numbers == 0, 1.0, 2.0) / length
    kept_mask = numbers.astype(jnp.float32)[None, :] < keep_values[:, None]
    return jnp.where(kept_mask, scaling[None, :], 0.0)


def lowpass_circles(circles, keep_piece):
    length = circles.shape[2]
    table_full = wave_table(length, length)
    coefficient = jnp.einsum("rqn,nk->rqk", circles, table_full, precision=lax.Precision.HIGHEST)
    keep_values = keep_piece[:, 0, 0]
    coefficient = coefficient * wave_weights(keep_values, length)[:, None, :]
    lowpass = jnp.einsum("rqk,nk->rqn", coefficient, table_full, precision=lax.Precision.HIGHEST)
    return jnp.where((keep_values <= KMAX)[:, None, None], lowpass, circles)


def smooth_polar(pieces):
    lowpass = lowpass_circles(pieces[0], pieces[1])
    return lax.all_to_all(lowpass, "lon", split_axis=2, concat_axis=1, tiled=True)


def filter_field(field, filter_keep):
    row_count = field.shape[0]
    lon_count = lax.axis_size("lon")
    polar_count = POLAR
    at_north_end = lax.axis_index("lat") == 0
    top_rows = field[:polar_count]
    bottom_rows = field[row_count - polar_count :]
    end_rows = jnp.where(at_north_end, top_rows, bottom_rows)
    end_keep = jnp.where(
        at_north_end, filter_keep[:polar_count], filter_keep[row_count - polar_count :]
    )
    reordered = jnp.transpose(end_rows, (0, 2, 1))
    keep_copies = jnp.broadcast_to(
        end_keep.astype(jnp.float32)[:, None, None], (polar_count, lon_count, 1)
    )
    smoothed = smooth_polar(
        (
            lax.all_to_all(reordered, "lon", split_axis=1, concat_axis=2, tiled=True),
            lax.all_to_all(keep_copies, "lon", split_axis=1, concat_axis=2, tiled=True),
        )
    )
    smoothed = jnp.transpose(smoothed, (0, 2, 1))
    new_top = jnp.where(at_north_end, smoothed, top_rows)
    new_bottom = jnp.where(at_north_end, bottom_rows, smoothed)
    return jnp.concatenate(
        [new_top, field[polar_count : row_count - polar_count], new_bottom], axis=0
    )


def local(
    tracer,
    east_courant,
    north_courant,
    east_limiter,
    north_limiter,
    filter_keep,
    seed_aerosol,
    volatility,
    cotangent,
):
    row_count = tracer.shape[0]
    channels = tracer.shape[2]
    levels = east_courant.shape[2]
    species = volatility.shape[0]
    first_row = lax.axis_index("lat") * row_count
    packed = jnp.concatenate([tracer, east_courant, east_limiter.astype(jnp.float32)], axis=2)
    widened = east_west(packed)
    east_speed = widened[:, :, channels : channels + levels]
    east_choice = widened[:, :, channels + levels :].astype(jnp.int32)

    def zonal_only(window):
        return zonal_window(window, east_speed, east_choice, species)

    after_east, east_back = jax.vjp(zonal_only, widened[:, :, :channels])
    stacked = jnp.concatenate(
        [after_east, north_courant, north_limiter.astype(jnp.float32)], axis=2
    )
    tall_window = north_south(stacked)
    north_speed = tall_window[:, :, channels : channels + levels]
    north_choice = tall_window[:, :, channels + levels :].astype(jnp.int32)

    def meridional_only(window):
        return meridional_window(window, north_speed, north_choice, first_row, species)

    after_north, north_back = jax.vjp(meridional_only, tall_window[:, :, :channels])
    filtered = filter_field(after_north, filter_keep)

    def chemistry(values):
        return partition(positive(values), seed_aerosol, volatility)

    particle, chem_back = jax.vjp(chemistry, filtered)
    adjoint_filtered = filter_field(chem_back(cotangent)[0], filter_keep)
    return (particle, fold_columns(east_back(fold_rows(north_back(adjoint_filtered)[0]))[0]))


def solution(mesh):
    in_specs = (
        P("lat", "lon", None),
        P("lat", "lon", None),
        P("lat", "lon", None),
        P("lat", "lon", None),
        P("lat", "lon", None),
        P("lat"),
        P("lat", "lon", None),
        P(),
        P("lat", "lon", None),
    )
    out_specs = (P("lat", "lon", None), P("lat", "lon", None))
    return jax.shard_map(local, mesh=mesh, in_specs=in_specs, out_specs=out_specs, check_vma=False)
```

profile of v0, /device:TPU:1, one launch (start us, length us, event | category | flops | bytes accessed | tf_op | source)
XLA Modules:
  0.0 384.8 jit_solution(76066904610606902)
XLA Ops:
  3.5 14.6 %collective-permute-start = (f32[4,2,928]{2,0,1:T(4,128)S(1)}, f32[4,2,928]{2,0,1:T(4,128)S(1)}, u32[]{:S(2)}, u32[]{:S(2)}) collective-permute-start(f32[4,2,928]{2,0,1:T(4,128)S(1)} %get-tuple-element.41), channel_id=1, source_target_pairs={{1,0},{2,1},{3,2},{4,3},{5,4},{6,5},{7,6},{8,7},{9,8},{10,9},{11,1... | collective-permute-start | bytes 89096 | tf_op jit(solution)/shard_map/ppermute | solution.py:23
  20.6 5.8 %collective-permute-done.1 = f32[4,2,928]{2,0,1:T(4,128)S(1)} collective-permute-done((f32[4,2,928]{2,0,1:T(4,128)S(1)}, f32[4,2,928]{2,0,1:T(4,128)S(1)}, u32[]{:S(2)}, u32[]{:S(2)}) %collective-permute-start.1) | collective-permute-done | bytes 29728 | tf_op jit(solution)/shard_map/ppermute | solution.py:21
  36.6 4.0 %collective-permute-start.2 = (f32[2,45,928]{2,0,1:T(2,128)}, f32[2,45,928]{2,0,1:T(2,128)S(1)}, u32[]{:S(2)}, u32[]{:S(2)}) collective-permute-start(f32[2,45,928]{2,0,1:T(2,128)} %copy.348), channel_id=1, source_target_pairs={{32,0},{64,32},{96,64},{128,96},{160,128},{192,160},{224,192},{256... | collective-permute-start | bytes 1002248 | tf_op jit(solution)/shard_map/ppermute | solution.py:23
  43.6 4.2 %all-to-all-start = ((f32[2,32,1]{0,2,1:T(1,128)}), f32[2,32,1]{0,2,1:T(1,128)S(1)}, u32[]{:S(2)}, u32[]{:S(2)}) async-start(f32[2,32,1]{0,2,1:T(1,128)} %broadcast_in_dim.115), calls=%async_computation | async-start | bytes 32768 | tf_op jit(solution)/shard_map/all_to_all | solution.py:188
  52.6 4.6 %eq.170 = pred[5,45,864]{2,1,0:T(8,128)(4,1)} reshape(pred[5,45,32,27]{3,2,1,0:T(8,128)(4,1)S(1)} %broadcast_in_dim.124) | data formatting | bytes 388800 | tf_op jit(solution)/shard_map/jvp()/eq | solution.py:38
  58.6 4.6 %eq.173 = pred[5,45,864]{2,1,0:T(8,128)(4,1)} reshape(pred[5,45,32,27]{3,2,1,0:T(8,128)(4,1)S(1)} %broadcast_in_dim.125) | data formatting | bytes 388800 | tf_op jit(solution)/shard_map/jvp()/eq | solution.py:38
  63.5 2.3 maximum_maximum_fusion
  65.8 2.5 broadcast_in_dim.123
  68.3 4.9 %reshape.128 = f32[5,45,864]{2,1,0:T(8,128)S(1)} reshape(f32[5,45,32,27]{3,2,1,0:T(8,128)} %broadcast_in_dim.123) | data formatting | bytes 1555200 | tf_op jit(solution)/shard_map/jvp()/reshape | solution.py:31
  76.7 3.0 reshape.142
  79.7 12.1 %all-to-all-start.1 = ((f32[32,1,2430]{2,1,0:T(1,128)}), f32[32,1,2430]{2,1,0:T(1,128)S(1)}, u32[]{:S(2)}, u32[]{:S(2)}) async-start(f32[32,1,2430]{2,1,0:T(1,128)} %reshape.142), calls=%async_computation.1 | async-start | bytes 622592 | tf_op jit(solution)/shard_map/all_to_all | solution.py:187
  93.0 22.6 %all-to-all-done.1 = f32[32,1,2430]{2,1,0:T(1,128)S(1)} async-done(((f32[32,1,2430]{2,1,0:T(1,128)}), f32[32,1,2430]{2,1,0:T(1,128)S(1)}, u32[]{:S(2)}, u32[]{:S(2)}) %all-to-all-start.1) | async-done | bytes 311072 | tf_op jit(solution)/shard_map/all_to_all | solution.py:187
  124.9 3.2 copy.360
  128.1 3.7 reshape.144
  131.8 5.0 %all-to-all-start.2 = ((f32[32,1,2430]{2,1,0:T(1,128)}), f32[32,1,2430]{2,1,0:T(1,128)S(1)}, u32[]{:S(2)}, u32[]{:S(2)}) async-start(f32[32,1,2430]{2,1,0:T(1,128)} %reshape.144), calls=%async_computation.2 | async-start | bytes 622592 | tf_op jit(solution)/shard_map/all_to_all | solution.py:167
  139.1 4.9 %reshape.129 = f32[4,45,864]{2,0,1:T(4,128)} reshape(f32[4,45,32,27]{3,2,0,1:T(8,128)} %broadcast_in_dim.130) | data formatting | bytes 1244160 | tf_op jit(solution)/shard_map/jvp()/reshape | solution.py:31
  144.0 15.2 %all-to-all-done.2 = f32[32,1,2430]{2,1,0:T(1,128)S(1)} async-done(((f32[32,1,2430]{2,1,0:T(1,128)}), f32[32,1,2430]{2,1,0:T(1,128)S(1)}, u32[]{:S(2)}, u32[]{:S(2)}) %all-to-all-start.2) | async-done | bytes 311072 | tf_op jit(solution)/shard_map/all_to_all | solution.py:167
  162.7 2.7 copy.542
  165.4 3.5 all_to_all.75
  175.1 5.3 %reshape.130 = f32[4,45,864]{2,0,1:T(4,128)} reshape(f32[4,45,32,27]{3,2,0,1:T(8,128)} %broadcast_in_dim.131) | data formatting | bytes 1244160 | tf_op jit(solution)/shard_map/jvp()/reshape | solution.py:31
  180.4 2.2 convolution_add_fusion.6
  186.6 4.9 %reshape.131 = f32[4,45,864]{2,0,1:T(4,128)} reshape(f32[4,45,32,27]{3,2,0,1:T(8,128)} %broadcast_in_dim.132) | data formatting | bytes 1244160 | tf_op jit(solution)/shard_map/jvp()/reshape | solution.py:31
  197.6 4.9 %reshape.132 = f32[4,45,864]{2,0,1:T(4,128)} reshape(f32[4,45,32,27]{3,2,0,1:T(8,128)} %broadcast_in_dim.133) | data formatting | bytes 1244160 | tf_op jit(solution)/shard_map/jvp()/reshape | solution.py:31
  202.5 2.2 convolution_add_fusion.4
  208.7 4.4 %reshape.133 = f32[4,45,864]{2,0,1:T(4,128)S(1)} reshape(f32[4,45,32,27]{3,2,0,1:T(8,128)} %broadcast_in_dim.134) | data formatting | bytes 1244160 | tf_op jit(solution)/shard_map/jvp()/reshape | solution.py:31
  213.1 2.6 multiply_add_fusion
  215.9 5.2 %reshape.134 = f32[4,45,32,27]{3,2,0,1:T(8,128)} reshape(f32[4,45,864]{2,0,1:T(4,128)S(1)} %copy.378) | data formatting | bytes 1244160 | tf_op jit(solution)/shard_map/transpose(jvp())/reshape | solution.py:31
  221.1 2.7 reduce_sum.36
  224.5 3.0 negate_add_fusion.2
  227.8 5.2 %reshape.135 = f32[4,45,32,27]{3,2,0,1:T(8,128)} reshape(f32[4,45,864]{2,0,1:T(4,128)S(1)} %copy.381) | data formatting | bytes 1244160 | tf_op jit(solution)/shard_map/transpose(jvp())/reshape | solution.py:31
  233.0 2.7 reduce_sum.37
  236.7 3.0 negate_add_fusion.1
  240.0 5.4 %reshape.136 = f32[4,45,32,27]{3,2,0,1:T(8,128)} reshape(f32[4,45,864]{2,0,1:T(4,128)S(1)} %copy.383) | data formatting | bytes 1244160 | tf_op jit(solution)/shard_map/transpose(jvp())/reshape | solution.py:31
  245.4 2.7 reduce_sum.38
  250.4 3.0 negate_add_fusion
  253.6 5.2 %reshape.137 = f32[4,45,32,27]{3,2,0,1:T(8,128)} reshape(f32[4,45,864]{2,0,1:T(4,128)S(1)} %copy.385) | data formatting | bytes 1244160 | tf_op jit(solution)/shard_map/transpose(jvp())/reshape | solution.py:31
  258.8 2.8 reduce_sum.39
  265.1 3.0 add_add_fusion
  271.2 28.4 %all_to_all.89 = f32[32,1,2430]{2,1,0:T(1,128)S(1)} all-to-all(f32[32,1,2430]{2,1,0:T(1,128)S(1)} %reshape.146), channel_id=1, replica_groups=mesh['lat'=16,'lon'=32] {'lon'}, dimensions={0} | all-to-all | bytes 622080 | tf_op jit(solution)/shard_map/all_to_all | solution.py:187
  307.6 3.0 reshape.148
  310.6 28.1 %all_to_all.90 = f32[32,1,2430]{2,1,0:T(1,128)S(1)} all-to-all(f32[32,1,2430]{2,1,0:T(1,128)S(1)} %reshape.148), channel_id=1, replica_groups=mesh['lat'=16,'lon'=32] {'lon'}, dimensions={0} | all-to-all | bytes 622080 | tf_op jit(solution)/shard_map/all_to_all | solution.py:167
  342.3 2.7 copy.541
  344.9 2.8 all_to_all.83
  350.3 8.4 %collective-permute-start.4 = (f32[2,45,864]{2,0,1:T(2,128)S(1)}, f32[2,45,864]{2,0,1:T(2,128)S(1)}, u32[]{:S(2)}, u32[]{:S(2)}) collective-permute-start(f32[2,45,864]{2,0,1:T(2,128)S(1)} %copy.396), channel_id=1, source_target_pairs={{0,32},{32,64},{64,96},{96,128},{128,160},{160,192},{192,224},{224... | collective-permute-start | bytes 933128 | tf_op jit(solution)/shard_map/ppermute | solution.py:21
  358.7 3.9 %collective-permute-done.4 = f32[2,45,864]{2,0,1:T(2,128)S(1)} collective-permute-done((f32[2,45,864]{2,0,1:T(2,128)S(1)}, f32[2,45,864]{2,0,1:T(2,128)S(1)}, u32[]{:S(2)}, u32[]{:S(2)}) %collective-permute-start.4) | collective-permute-done | bytes 311072 | tf_op jit(solution)/shard_map/ppermute | solution.py:21
  366.2 5.8 %collective-permute-done.5 = f32[2,45,864]{2,0,1:T(2,128)S(1)} collective-permute-done((f32[2,45,864]{2,0,1:T(2,128)S(1)}, f32[2,45,864]{2,0,1:T(2,128)S(1)}, u32[]{:S(2)}, u32[]{:S(2)}) %collective-permute-start.5) | collective-permute-done | bytes 311072 | tf_op jit(solution)/shard_map/ppermute | solution.py:23
  375.0 3.4 collective-permute-start.6
  379.0 4.2 %collective-permute-done.6 = f32[4,2,864]{2,0,1:T(4,128)S(1)} collective-permute-done((f32[4,2,864]{2,0,1:T(4,128)S(1)}, f32[4,2,864]{2,0,1:T(4,128)S(1)}, u32[]{:S(2)}, u32[]{:S(2)}) %collective-permute-start.6) | collective-permute-done | bytes 27680 | tf_op jit(solution)/shard_map/ppermute | solution.py:21
  (266 shorter events, 97.9 us)
Async XLA Ops:
  0.6 19.6 %copy-start = (f32[4,45,864]{2,0,1:T(4,128)S(1)}, f32[4,45,864]{2,0,1:T(4,128)}, u32[]{:S(2)}) copy-start(f32[4,45,864]{2,0,1:T(4,128)} %param.9) | copy-start | bytes 1866244
  0.6 19.4 %copy-start.50 = (s32[4,45,32]{1,2,0:T(8,128)S(1)}, s32[4,45,32]{1,2,0:T(8,128)}, u32[]{:S(2)}) copy-start(s32[4,45,32]{1,2,0:T(8,128)} %param.13) | copy-start | bytes 69124
  0.7 19.5 %copy-start.51 = (f32[4,45,32]{1,2,0:T(8,128)S(1)}, f32[4,45,32]{1,2,0:T(8,128)}, u32[]{:S(2)}) copy-start(f32[4,45,32]{1,2,0:T(8,128)} %param.11) | copy-start | bytes 69124
  3.5 16.8 %collective-permute-start = (f32[4,2,928]{2,0,1:T(4,128)S(1)}, f32[4,2,928]{2,0,1:T(4,128)S(1)}, u32[]{:S(2)}, u32[]{:S(2)}) collective-permute-start(f32[4,2,928]{2,0,1:T(4,128)S(1)} %get-tuple-element.41), channel_id=1, source_target_pairs={{1,0},{2,1},{3,2},{4,3},{5,4},{6,5},{7,6},{8,7},{9,8},{10,9},{11,1... | collective-permute-start | bytes 89096 | tf_op jit(solution)/shard_map/ppermute | solution.py:23
  18.1 8.3 %collective-permute-start.1 = (f32[4,2,928]{2,0,1:T(4,128)S(1)}, f32[4,2,928]{2,0,1:T(4,128)S(1)}, u32[]{:S(2)}, u32[]{:S(2)}) collective-permute-start(f32[4,2,928]{2,0,1:T(4,128)S(1)} %get-tuple-element.40), channel_id=1, source_target_pairs={{0,1},{1,2},{2,3},{3,4},{4,5},{5,6},{6,7},{7,8},{8,9},{9,10},{10,1... | collective-permute-start | bytes 89096 | tf_op jit(solution)/shard_map/ppermute | solution.py:21
  20.3 43.0 %copy-start.10 = (f32[4,45,32]{2,1,0:T(8,128)}, f32[4,45,32]{2,1,0:T(8,128)S(1)}, u32[]{:S(2)}) copy-start(f32[4,45,32]{2,1,0:T(8,128)S(1)} %copy.346) | copy-start | bytes 69124
  28.1 5.8 %copy-start.6 = (pred[4,46,864]{2,1,0:T(8,128)(4,1)}, pred[4,46,864]{2,1,0:T(8,128)(4,1)S(1)}, u32[]{:S(2)}) copy-start(pred[4,46,864]{2,1,0:T(8,128)(4,1)S(1)} %copy.343) | copy-start | bytes 476932
  29.5 4.4 %copy-start.8 = (pred[4,46,864]{2,1,0:T(8,128)(4,1)}, pred[4,46,864]{2,1,0:T(8,128)(4,1)S(1)}, u32[]{:S(2)}) copy-start(pred[4,46,864]{2,1,0:T(8,128)(4,1)S(1)} %copy.342) | copy-start | bytes 476932
  34.5 8.4 %copy-start.58 = (s32[4]{0:T(128)S(1)}, s32[4]{0:T(128)}, u32[]{:S(2)}) copy-start(s32[4]{0:T(128)} %param.14) | copy-start | bytes 52
  36.6 11.7 %collective-permute-start.2 = (f32[2,45,928]{2,0,1:T(2,128)}, f32[2,45,928]{2,0,1:T(2,128)S(1)}, u32[]{:S(2)}, u32[]{:S(2)}) collective-permute-start(f32[2,45,928]{2,0,1:T(2,128)} %copy.348), channel_id=1, source_target_pairs={{32,0},{64,32},{96,64},{128,96},{160,128},{192,160},{224,192},{256... | collective-permute-start | bytes 1002248 | tf_op jit(solution)/shard_map/ppermute | solution.py:23
  40.6 9.9 %collective-permute-start.3 = (f32[2,45,928]{2,0,1:T(2,128)}, f32[2,45,928]{2,0,1:T(2,128)S(1)}, u32[]{:S(2)}, u32[]{:S(2)}) collective-permute-start(f32[2,45,928]{2,0,1:T(2,128)} %copy.350), channel_id=1, source_target_pairs={{0,32},{32,64},{64,96},{96,128},{128,160},{160,192},{192,224},{224... | collective-permute-start | bytes 1002248 | tf_op jit(solution)/shard_map/ppermute | solution.py:21
  43.6 36.1 %all-to-all-start = ((f32[2,32,1]{0,2,1:T(1,128)}), f32[2,32,1]{0,2,1:T(1,128)S(1)}, u32[]{:S(2)}, u32[]{:S(2)}) async-start(f32[2,32,1]{0,2,1:T(1,128)} %broadcast_in_dim.115), calls=%async_computation | async-start | bytes 32768 | tf_op jit(solution)/shard_map/all_to_all | solution.py:188
  52.6 10.5 %copy-start.12 = (f32[2,45,928]{2,0,1:T(2,128)S(1)}, f32[2,45,928]{2,0,1:T(2,128)}, u32[]{:S(2)}) copy-start(f32[2,45,928]{2,0,1:T(2,128)} %copy-done.11) | copy-start | bytes 1002244
  58.5 4.9 %copy-start.14 = (f32[2,45,928]{2,0,1:T(2,128)S(1)}, f32[2,45,928]{2,0,1:T(2,128)}, u32[]{:S(2)}) copy-start(f32[2,45,928]{2,0,1:T(2,128)} %copy-done.13) | copy-start | bytes 1002244
  79.7 35.9 %all-to-all-start.1 = ((f32[32,1,2430]{2,1,0:T(1,128)}), f32[32,1,2430]{2,1,0:T(1,128)S(1)}, u32[]{:S(2)}, u32[]{:S(2)}) async-start(f32[32,1,2430]{2,1,0:T(1,128)} %reshape.142), calls=%async_computation.1 | async-start | bytes 622592 | tf_op jit(solution)/shard_map/all_to_all | solution.py:187
  92.9 30.7 %copy-start.56 = (pred[2]{0:T(512)(128)(4,1)}, pred[2]{0:T(512)(128)(4,1)S(1)}, u32[]{:S(2)}) copy-start(pred[2]{0:T(512)(128)(4,1)S(1)} %compare_reduce_fusion) | copy-start | bytes 10
  93.0 30.1 %copy-start.54 = (f32[2,64]{1,0:T(2,128)}, f32[2,64]{1,0:T(2,128)S(1)}, u32[]{:S(2)}) copy-start(f32[2,64]{1,0:T(2,128)S(1)} %compare_select_fusion.1) | copy-start | bytes 1540
  128.1 8.7 %copy-start.59 = (f32[27]{0:T(128)S(1)}, f32[27]{0:T(128)}, u32[]{:S(2)}) copy-start(f32[27]{0:T(128)} %param.16) | copy-start | bytes 328
  128.1 8.8 %copy-start.23 = (f32[4,45,32]{1,2,0:T(8,128)S(1)}, f32[4,45,32]{1,2,0:T(8,128)}, u32[]{:S(2)}) copy-start(f32[4,45,32]{1,2,0:T(8,128)} %param.15) | copy-start | bytes 69124
  131.8 27.4 %all-to-all-start.2 = ((f32[32,1,2430]{2,1,0:T(1,128)}), f32[32,1,2430]{2,1,0:T(1,128)S(1)}, u32[]{:S(2)}, u32[]{:S(2)}) async-start(f32[32,1,2430]{2,1,0:T(1,128)} %reshape.144), calls=%async_computation.2 | async-start | bytes 622592 | tf_op jit(solution)/shard_map/all_to_all | solution.py:167
  136.9 87.6 %copy-start.52 = (f32[864]{0:T(1024)}, f32[864]{0:T(1024)S(1)}, u32[]{:S(2)}) copy-start(f32[864]{0:T(1024)S(1)} %add.158) | copy-start | bytes 10372
  170.0 43.1 %copy-start.15 = (f32[2,45,864]{2,1,0:T(8,128)}, f32[2,45,864]{2,1,0:T(8,128)S(1)}, u32[]{:S(2)}) copy-start(f32[2,45,864]{2,1,0:T(8,128)S(1)} %get-tuple-element.32) | copy-start | bytes 933124
  172.9 9.8 %copy-start.45 = (f32[4,45,32]{1,2,0:T(8,128)}, f32[4,45,32]{1,2,0:T(8,128)S(1)}, u32[]{:S(2)}) copy-start(f32[4,45,32]{1,2,0:T(8,128)S(1)} %get-tuple-element.54) | copy-start | bytes 69124
  175.1 5.3 %copy-start.21 = (f32[2,45,864]{2,1,0:T(8,128)S(1)}, f32[2,45,864]{2,1,0:T(8,128)}, u32[]{:S(2)}) copy-start(f32[2,45,864]{2,1,0:T(8,128)} %copy-done.20) | copy-start | bytes 933124
  184.4 9.3 %copy-start.46 = (f32[4,45,32]{1,2,0:T(8,128)}, f32[4,45,32]{1,2,0:T(8,128)S(1)}, u32[]{:S(2)}) copy-start(f32[4,45,32]{1,2,0:T(8,128)S(1)} %get-tuple-element.56) | copy-start | bytes 69124
  193.7 42.7 %copy-start.36 = (f32[4,45,32]{1,2,0:T(8,128)}, f32[4,45,32]{1,2,0:T(8,128)S(1)}, u32[]{:S(2)}) copy-start(f32[4,45,32]{1,2,0:T(8,128)S(1)} %convolution_add_fusion.5) | copy-start | bytes 69124
  195.4 9.3 %copy-start.48 = (f32[4,45,32]{1,2,0:T(8,128)}, f32[4,45,32]{1,2,0:T(8,128)S(1)}, u32[]{:S(2)}) copy-start(f32[4,45,32]{1,2,0:T(8,128)S(1)} %get-tuple-element.58) | copy-start | bytes 69124
  221.1 3.4 copy-start.16
  233.0 2.9 copy-start.42
  233.0 2.9 copy-start.44
  233.0 2.9 copy-start.49
  233.0 3.0 copy-start.38
  245.4 3.5 copy-start.37
  245.4 3.5 copy-start.39
  245.4 3.5 copy-start.47
  245.4 4.4 %copy-start.33 = (f32[4,45,32]{1,2,0:T(8,128)S(1)}, f32[4,45,32]{1,2,0:T(8,128)}, u32[]{:S(2)}) copy-start(f32[4,45,32]{1,2,0:T(8,128)} %copy-done.32) | copy-start | bytes 69124
  245.4 4.4 %copy-start.35 = (f32[4,45,32]{1,2,0:T(8,128)S(1)}, f32[4,45,32]{1,2,0:T(8,128)}, u32[]{:S(2)}) copy-start(f32[4,45,32]{1,2,0:T(8,128)} %get-tuple-element.57) | copy-start | bytes 69124
  258.8 3.5 copy-start.34
  258.8 4.5 %copy-start.26 = (f32[4,45,864]{2,0,1:T(4,128)S(1)}, f32[4,45,864]{2,0,1:T(4,128)}, u32[]{:S(2)}) copy-start(f32[4,45,864]{2,0,1:T(4,128)} %reshape.129) | copy-start | bytes 1866244
  258.8 4.5 %copy-start.53 = (f32[864]{0:T(1024)S(1)}, f32[864]{0:T(1024)}, u32[]{:S(2)}) copy-start(f32[864]{0:T(1024)} %copy-done.52) | copy-start | bytes 10372
  301.6 3.0 copy-start.55
  350.1 15.0 %copy-start.3 = (f32[4,45,864]{2,1,0:T(8,128)S(1)}, f32[4,45,864]{2,1,0:T(8,128)}, u32[]{:S(2)}) copy-start(f32[4,45,864]{2,1,0:T(8,128)} %get-tuple-element.27) | copy-start | bytes 1866244
  350.3 12.4 %collective-permute-start.4 = (f32[2,45,864]{2,0,1:T(2,128)S(1)}, f32[2,45,864]{2,0,1:T(2,128)S(1)}, u32[]{:S(2)}, u32[]{:S(2)}) collective-permute-start(f32[2,45,864]{2,0,1:T(2,128)S(1)} %copy.396), channel_id=1, source_target_pairs={{0,32},{32,64},{64,96},{96,128},{128,160},{160,192},{192,224},{224... | collective-permute-start | bytes 933128 | tf_op jit(solution)/shard_map/ppermute | solution.py:21
  362.9 9.1 %collective-permute-start.5 = (f32[2,45,864]{2,0,1:T(2,128)S(1)}, f32[2,45,864]{2,0,1:T(2,128)S(1)}, u32[]{:S(2)}, u32[]{:S(2)}) collective-permute-start(f32[2,45,864]{2,0,1:T(2,128)S(1)} %copy.398), channel_id=1, source_target_pairs={{32,0},{64,32},{96,64},{128,96},{160,128},{192,160},{224,192},{256... | collective-permute-start | bytes 933128 | tf_op jit(solution)/shard_map/ppermute | solution.py:23
  366.2 5.9 %copy-start.7 = (pred[4,46,864]{2,1,0:T(8,128)(4,1)S(1)}, pred[4,46,864]{2,1,0:T(8,128)(4,1)}, u32[]{:S(2)}) copy-start(pred[4,46,864]{2,1,0:T(8,128)(4,1)} %copy-done.6) | copy-start | bytes 476932
  366.2 5.9 %copy-start.9 = (pred[4,46,864]{2,1,0:T(8,128)(4,1)S(1)}, pred[4,46,864]{2,1,0:T(8,128)(4,1)}, u32[]{:S(2)}) copy-start(pred[4,46,864]{2,1,0:T(8,128)(4,1)} %copy-done.8) | copy-start | bytes 476932
  373.0 6.0 %collective-permute-start.7 = (f32[4,2,864]{2,0,1:T(4,128)S(1)}, f32[4,2,864]{2,0,1:T(4,128)S(1)}, u32[]{:S(2)}, u32[]{:S(2)}) collective-permute-start(f32[4,2,864]{2,0,1:T(4,128)S(1)} %copy.407), channel_id=1, source_target_pairs={{1,0},{2,1},{3,2},{4,3},{5,4},{6,5},{7,6},{8,7},{9,8},{10,9},{11,1... | collective-permute-start | bytes 82952 | tf_op jit(solution)/shard_map/ppermute | solution.py:23
  375.0 8.2 %collective-permute-start.6 = (f32[4,2,864]{2,0,1:T(4,128)S(1)}, f32[4,2,864]{2,0,1:T(4,128)S(1)}, u32[]{:S(2)}, u32[]{:S(2)}) collective-permute-start(f32[4,2,864]{2,0,1:T(4,128)S(1)} %copy.405), channel_id=1, source_target_pairs={{0,1},{1,2},{2,3},{3,4},{4,5},{5,6},{6,7},{7,8},{8,9},{9,10},{10,1... | collective-permute-start | bytes 82952 | tf_op jit(solution)/shard_map/ppermute | solution.py:21
  (25 other events, 44.2 us)
where the time goes:
time: 391 us; the launch traced here: 385 us
  local copies, waits for them, and re-layouts  139 us (36%)
  starting transfers between devices  59.9 us (15%)
  waiting for transfers between devices  59.7 us (15%)
  blocking collectives  56.5 us (14%)
  other arithmetic  34.5 us (9%)
  matrix products  32.3 us (8%)
    reshape x11, local copies, waits for them, and re-layouts, spread(): return jnp.repeat(values, copies, axis=-1)  52.3 us
    all_to_all x1, blocking collectives, filter_field(): lax.all_to_all(reordered, 'lon', split_axis=1, concat_axis=2, tiled=True)  28.4 us
    all_to_all x1, blocking collectives, smooth_polar(): lax.all_to_all(lowpass, 'lon', split_axis=2, concat_axis=1, tiled=True)  28.1 us
    unnamed x137, local copies, waits for them, and re-layouts  23 us
    ppermute x4, starting transfers between devices, with_halo(): lax.ppermute(head, axis, [((i + 1) % count, i) for i in range(ends)])  22.7 us
    all_to_all x1, waiting for transfers between devices, filter_field(): lax.all_to_all(reordered, 'lon', split_axis=1, concat_axis=2, tiled=True)  22.6 us
    dot_general x8, matrix products, partition(): first_sum = jnp.dot(fraction, grouping, precision=lax.Precision.HIGHEST)  18.8 us
    broadcast_in_dim x11, local copies, waits for them, and re-layouts, spread(): return jnp.repeat(values, copies, axis=-1)  17.5 us
  transfers between devices with their start and end apart: 11, of which 7 were waited for; matrix products, arithmetic and copies ran while one was open for 10% of the time, Pallas kernels for 0%

commit v1 on v0

--- a/solution.py
+++ b/solution.py
@@ -4,6 +4,8 @@
 import jax.numpy as jnp
 from jax import lax
 from jax.sharding import PartitionSpec as P
+from jax.experimental import pallas as pl
+from jax.experimental.pallas import tpu as pltpu
 
 NEWTON = 4
 KMAX = 32
@@ -137,10 +139,9 @@
     )
 
 
-def wave_table(column_count, length):
-    position = jnp.arange(column_count, dtype=jnp.int32)
+def wave_table(positions, length):
     numbers = jnp.arange(KMAX, dtype=jnp.int32)
-    phases = position[:, None] * numbers[None, :] % length
+    phases = positions[:, None] * numbers[None, :] % length
     angles = phases.astype(jnp.float32) * (2.0 * math.pi / length)
     return jnp.concatenate([jnp.cos(angles), jnp.sin(angles)], axis=1)
 
@@ -148,28 +149,13 @@
 def wave_weights(keep_values, length):
     numbers = jnp.arange(2 * KMAX, dtype=jnp.int32) % KMAX
     scaling = jnp.where(numbers == 0, 1.0, 2.0) / length
-    kept_mask = numbers.astype(jnp.float32)[None, :] < keep_values[:, None]
+    kept_mask = numbers[None, :] < keep_values[:, None]
     return jnp.where(kept_mask, scaling[None, :], 0.0)
 
 
-def lowpass_circles(circles, keep_piece):
-    length = circles.shape[2]
-    table_full = wave_table(length, length)
-    coefficient = jnp.einsum("rqn,nk->rqk", circles, table_full, precision=lax.Precision.HIGHEST)
-    keep_values = keep_piece[:, 0, 0]
-    coefficient = coefficient * wave_weights(keep_values, length)[:, None, :]
-    lowpass = jnp.einsum("rqk,nk->rqn", coefficient, table_full, precision=lax.Precision.HIGHEST)
-    return jnp.where((keep_values <= KMAX)[:, None, None], lowpass, circles)
-
-
-def smooth_polar(pieces):
-    lowpass = lowpass_circles(pieces[0], pieces[1])
-    return lax.all_to_all(lowpass, "lon", split_axis=2, concat_axis=1, tiled=True)
-
-
 def filter_field(field, filter_keep):
-    row_count = field.shape[0]
-    lon_count = lax.axis_size("lon")
+    row_count, col_count = field.shape[0], field.shape[1]
+    length = col_count * lax.axis_size("lon")
     polar_count = POLAR
     at_north_end = lax.axis_index("lat") == 0
     top_rows = field[:polar_count]
@@ -178,22 +164,92 @@
     end_keep = jnp.where(
         at_north_end, filter_keep[:polar_count], filter_keep[row_count - polar_count :]
     )
-    reordered = jnp.transpose(end_rows, (0, 2, 1))
-    keep_copies = jnp.broadcast_to(
-        end_keep.astype(jnp.float32)[:, None, None], (polar_count, lon_count, 1)
-    )
-    smoothed = smooth_polar(
-        (
-            lax.all_to_all(reordered, "lon", split_axis=1, concat_axis=2, tiled=True),
-            lax.all_to_all(keep_copies, "lon", split_axis=1, concat_axis=2, tiled=True),
-        )
-    )
-    smoothed = jnp.transpose(smoothed, (0, 2, 1))
+    positions = lax.axis_index("lon") * col_count + jnp.arange(col_count, dtype=jnp.int32)
+    table = wave_table(positions, length)
+    hi = lax.Precision.HIGHEST
+    partial = jnp.einsum("rjq,jk->rkq", end_rows, table, precision=hi)
+    coefficient = lax.psum(partial, "lon")
+    coefficient = coefficient * wave_weights(end_keep, length)[:, :, None]
+    lowpass = jnp.einsum("jk,rkq->rjq", table, coefficient, precision=hi)
+    smoothed = jnp.where((end_keep <= KMAX)[:, None, None], lowpass, end_rows)
     new_top = jnp.where(at_north_end, smoothed, top_rows)
     new_bottom = jnp.where(at_north_end, bottom_rows, smoothed)
     return jnp.concatenate(
         [new_top, field[polar_count : row_count - polar_count], new_bottom], axis=0
     )
+
+
+def chem_kernel(x_ref, seed_ref, cot_ref, sat_ref, spread_ref, group_ref, p_ref, g_ref):
+    hi = lax.Precision.HIGHEST
+    x = x_ref[0]
+    seed = seed_ref[0]
+    cot = cot_ref[0]
+    sat = sat_ref[...]
+    spread_m = spread_ref[...]
+    group_m = group_ref[...]
+
+    def up(v):
+        return jnp.dot(v, spread_m, precision=hi, preferred_element_type=jnp.float32)
+
+    def down(v):
+        return jnp.dot(v, group_m, precision=hi, preferred_element_type=jnp.float32)
+
+    root = jnp.sqrt(x * x + 1.0)
+    mass = 0.5 * (x + root)
+    aerosol = seed
+    history = []
+    for newton_step in range(NEWTON):
+        denominator = up(aerosol) + sat
+        fraction = mass / denominator
+        first_sum = down(fraction)
+        second_sum = down(fraction / denominator)
+        residue = 1.0 - seed / aerosol - first_sum
+        derivative = seed / (aerosol * aerosol) + second_sum
+        history.append((aerosol, residue, derivative))
+        aerosol = aerosol - residue / derivative
+    aerosol_q = up(aerosol)
+    final_den = aerosol_q + sat
+    p_ref[0] = mass * aerosol_q / final_den
+    mass_bar = cot * aerosol_q / final_den
+    aerosol_bar = down(cot * mass * sat / (final_den * final_den))
+    for newton_step in reversed(range(NEWTON)):
+        a_n, residue, derivative = history[newton_step]
+        inverse = 1.0 / (up(a_n) + sat)
+        third_sum = down(mass * inverse * inverse * inverse)
+        slope = -2.0 * (seed / (a_n * a_n * a_n) + third_sum)
+        over_g = aerosol_bar / derivative
+        over_g2 = over_g * residue / derivative
+        mass_bar = mass_bar + up(over_g) * inverse + up(over_g2) * inverse * inverse
+        aerosol_bar = over_g2 * slope
+    g_ref[0] = mass_bar * 0.5 * (1.0 + x / root)
+
+
+def chemistry_step(filtered, seed_aerosol, volatility, cotangent):
+    rows, cols, channels = filtered.shape
+    levels = seed_aerosol.shape[-1]
+    species = volatility.shape[0]
+    group_m = level_table(levels, species)
+    spread_m = group_m.T
+    sat = jnp.tile(volatility, levels)[None, :]
+    big = pl.BlockSpec((1, cols, channels), lambda i: (i, 0, 0))
+    small = pl.BlockSpec((1, cols, levels), lambda i: (i, 0, 0))
+    return pl.pallas_call(
+        chem_kernel,
+        grid=(rows,),
+        in_specs=[
+            big,
+            small,
+            big,
+            pl.BlockSpec((1, channels), lambda i: (0, 0)),
+            pl.BlockSpec((levels, channels), lambda i: (0, 0)),
+            pl.BlockSpec((channels, levels), lambda i: (0, 0)),
+        ],
+        out_specs=[big, big],
+        out_shape=[
+            jax.ShapeDtypeStruct(filtered.shape, jnp.float32),
+            jax.ShapeDtypeStruct(filtered.shape, jnp.float32),
+        ],
+    )(filtered, seed_aerosol, cotangent, sat, spread_m, group_m)
 
 
 def local(
@@ -234,11 +290,8 @@
     after_north, north_back = jax.vjp(meridional_only, tall_window[:, :, :channels])
     filtered = filter_field(after_north, filter_keep)
 
-    def chemistry(values):
-        return partition(positive(values), seed_aerosol, volatility)
-
-    particle, chem_back = jax.vjp(chemistry, filtered)
-    adjoint_filtered = filter_field(chem_back(cotangent)[0], filter_keep)
+    particle, chem_grad = chemistry_step(filtered, seed_aerosol, volatility, cotangent)
+    adjoint_filtered = filter_field(chem_grad, filter_keep)
     return (particle, fold_columns(east_back(fold_rows(north_back(adjoint_filtered)[0]))[0]))
 
 

time: 391 us -> 729 us (1.86)
  waiting for transfers between devices: 59.7 us -> 573 us
  local copies, waits for them, and re-layouts: 139 us -> 35.5 us
  blocking collectives: 56.5 us -> 0 us
  matrix products: 32.3 us -> 7.04 us
  Pallas kernels: 0 us -> 23.7 us
  other arithmetic: 34.5 us -> 15.2 us
  between operations: 2.54 us -> 14.7 us
    psum x0 -> x2, waiting for transfers between devices: none -> 559 us  [filter_field(): coefficient = lax.psum(partial, 'lon')]
    all_to_all x2 -> x0, blocking collectives: 56.5 us -> none  [the longest x1 28.4 us: filter_field(): lax.all_to_all(reordered, 'lon', split_axis=1, concat_axis=2, tiled=True)]
    reshape x11 -> x2, local copies, waits for them, and re-layouts: 52.3 us -> 5.82 us  [spread(): return jnp.repeat(values, copies, axis=-1)]
    all_to_all x3 -> x0, waiting for transfers between devices: 37.8 us -> none  [the longest x1 22.6 us: filter_field(): lax.all_to_all(reordered, 'lon', split_axis=1, concat_axis=2, tiled=True)]
    dot_general x20 -> x4, matrix products: 32.3 us -> 7.04 us  [the longest x2 3.84 us: filter_field(): partial = jnp.einsum('rjq,jk->rkq', end_rows, table, precision=hi)]
    pallas_call x0 -> x1, Pallas kernels: none -> 23.7 us  [chemistry_step(): pl.pallas_call(chem_kernel, grid=(rows,), in_specs=[big, small, big, pl.B...]
    all_to_all x3 -> x0, starting transfers between devices: 21.3 us -> none  [the longest x1 12.1 us: filter_field(): lax.all_to_all(reordered, 'lon', split_axis=1, concat_axis=2, tiled=True)]
    all_to_all x10 -> x0, local copies, waits for them, and re-layouts: 19.3 us -> none  [the longest x4 11.7 us: smooth_polar(): lax.all_to_all(lowpass, 'lon', split_axis=2, concat_axis=1, tiled=True)]
  transfers between devices with their start and end apart: 11 -> 10, of which waited for: 7 -> 6; matrix products, arithmetic and copies ran while one was open for 10% -> 2% of each run, Pallas kernels for 0% -> 0%
where the time goes in v1:
time: 729 us; the launch traced here: 727 us
  waiting for transfers between devices  573 us (79%)
  starting transfers between devices  57.9 us (8%)
  local copies, waits for them, and re-layouts  35.5 us (5%)
  Pallas kernels  23.7 us (3%)
  other arithmetic  15.2 us (2%)
  between operations  14.7 us (2%)
    psum x2, waiting for transfers between devices, filter_field(): coefficient = lax.psum(partial, 'lon')  559 us
    ppermute x4, starting transfers between devices, with_halo(): lax.ppermute(tail, axis, [(i, (i + 1) % count) for i in range(ends)])  30.9 us
    ppermute x4, starting transfers between devices, with_halo(): lax.ppermute(head, axis, [((i + 1) % count, i) for i in range(ends)])  26.9 us
    pallas_call x1, Pallas kernels, chemistry_step(): pl.pallas_call(chem_kernel, grid=(rows,), in_specs=[big, small, big, pl.B...  23.7 us
  transfers between devices with their start and end apart: 10, of which 6 were waited for; matrix products, arithmetic and copies ran while one was open for 2% of the time, Pallas kernels for 0%

profile of v1, /device:TPU:1, one launch (start us, length us, event | category | flops | bytes accessed | tf_op | source)
XLA Modules:
  0.0 726.8 jit_solution(7120095165371410569)
XLA Ops:
  7.2 0.8 convert_element_type.22
  8.2 1.0 copy.44
  9.1 1.2 copy.55
  10.3 0.7 pad_maximum_fusion.16
  11.0 14.7 %collective-permute-start = (f32[4,2,928]{2,1,0:T(2,128)S(1)}, f32[4,2,928]{2,1,0:T(2,128)S(1)}, u32[]{:S(2)}, u32[]{:S(2)}) collective-permute-start(f32[4,2,928]{2,1,0:T(2,128)S(1)} %get-tuple-element.39), channel_id=1, source_target_pairs={{1,0},{2,1},{3,2},{4,3},{5,4},{6,5},{7,6},{8,7},{9,8},{10,9},{11,1... | collective-permute-start | bytes 89096 | tf_op jit(solution)/shard_map/ppermute | solution.py:25
  25.7 1.9 collective-permute-start.1
  28.4 0.7 fusion.18.spread_ref
  29.1 0.7 maximum_bitcast_fusion
  30.6 0.7 copy.58.seed_ref
  31.4 0.9 copy.59.cot_ref
  32.3 0.7 broadcast_in_dim_tile.3.sat_ref
  33.6 1.3 copy.54
  35.0 0.8 broadcast_compare_fusion.4
  36.2 1.2 copy.53
  37.8 1.2 copy.52
  39.0 1.0 maximum_maximum_fusion.1
  40.5 0.6 copy-done.6
  41.4 0.8 fusion.35
  42.2 3.3 collective-permute-start.2
  46.1 2.4 collective-permute-start.3
  48.5 2.7 collective-permute-done.2
  51.4 2.4 broadcast_in_dim.96
  53.9 4.5 reshape.101
  58.4 0.7 broadcast_compare_fusion.2
  59.1 1.3 broadcast_in_dim.97
  60.5 4.6 eq.87
  65.0 3.1 broadcast_in_dim.98
  68.1 4.6 eq.90
  72.7 1.6 maximum_maximum_fusion
  74.9 0.6 copy-done.15
  75.5 1.3 convolution_bitcast_fusion.1
  77.0 0.9 fusion.14.group_ref
  78.0 271.6 %all-reduce.17.cloned.1.call-done = f32[2,64,864]{2,1,0:T(8,128)} async-done(((f32[2,64,864]{2,1,0:T(8,128)}), f32[2,64,864]{2,1,0:T(8,128)}) %all-reduce.17.cloned.1.call-update) | async-done | bytes 442384 | tf_op jit(solution)/shard_map/psum | solution.py:171
  349.6 1.6 slice_select_fusion.2
  351.2 0.9 pad_maximum_fusion.3.x_ref
  352.1 23.7 %shard_map.104 = (f32[4,45,864]{2,1,0:T(8,128)}, f32[4,45,864]{2,1,0:T(8,128)}) custom-call(f32[4,45,864]{2,1,0:T(8,128)} %pad_maximum_fusion.3.x_ref, f32[4,45,32]{2,1,0:T(8,128)} %copy.58.seed_ref, f32[4,45,864]{2,1,0:T(8,128)} %copy.59.cot_ref, f32[1,864]{1,0:T(1,128)} %broadcast_in_dim_tile.3.sat_ref, f32[32,864]{1,0:T(8,128)} %fusion.18.spread_ref, ...), custom_call_target="tpu_custom_call" | custom-call | tf_op jit(solution)/shard_map/pallas_call | solution.py:236
  375.8 2.5 convolution_bitcast_fusion
  378.3 287.4 %all-reduce.19.cloned.1.call-done = f32[2,64,864]{2,1,0:T(8,128)} async-done(((f32[2,64,864]{2,1,0:T(8,128)}), f32[2,64,864]{2,1,0:T(8,128)}) %all-reduce.19.cloned.1.call-update) | async-done | bytes 442384 | tf_op jit(solution)/shard_map/psum | solution.py:171
  665.7 1.6 slice_select_fusion.5
  668.6 24.7 %collective-permute-start.4 = (f32[2,45,864]{2,1,0:T(8,128)S(1)}, f32[2,45,864]{2,1,0:T(8,128)S(1)}, u32[]{:S(2)}, u32[]{:S(2)}) collective-permute-start(f32[2,45,864]{2,1,0:T(8,128)S(1)} %slice.204), channel_id=1, source_target_pairs={{0,32},{32,64},{64,96},{96,128},{128,160},{160,192},{192,224},{224... | collective-permute-start | bytes 933128 | tf_op jit(solution)/shard_map/ppermute | solution.py:23
  693.3 4.2 collective-permute-done.4
  697.6 1.9 collective-permute-start.5
  699.5 1.1 copy.65
  700.6 6.3 collective-permute-done.5
  707.0 0.8 copy-done.3
  708.8 1.9 collective-permute-start.6
  710.7 7.0 collective-permute-start.7
  718.9 1.1 copy.66
  (103 shorter events, 8.8 us)
Async XLA Ops:
  7.2 342.4 %all-reduce.17.cloned.1.call-start = ((), (), s32[]{:S(2)}) async-start(), calls=%async_computation | async-start | bytes 917504 | tf_op jit(solution)/shard_map/psum | solution.py:171
  9.1 21.3 %copy-start.18 = (s32[4,45,32]{1,2,0:T(8,128)S(1)}, s32[4,45,32]{1,2,0:T(8,128)}, u32[]{:S(2)}) copy-start(s32[4,45,32]{1,2,0:T(8,128)} %param.13) | copy-start | bytes 69124
  9.1 21.4 %copy-start.19 = (f32[4,45,32]{1,2,0:T(8,128)S(1)}, f32[4,45,32]{1,2,0:T(8,128)}, u32[]{:S(2)}) copy-start(f32[4,45,32]{1,2,0:T(8,128)} %param.11) | copy-start | bytes 69124
  9.1 21.5 %copy-start.20 = (f32[4,45,32]{1,2,0:T(8,128)S(1)}, f32[4,45,32]{1,2,0:T(8,128)}, u32[]{:S(2)}) copy-start(f32[4,45,32]{1,2,0:T(8,128)} %param.15) | copy-start | bytes 69124
  10.3 21.1 %copy-start.14 = (f32[4,45,864]{2,0,1:T(4,128)S(1)}, f32[4,45,864]{2,0,1:T(4,128)}, u32[]{:S(2)}) copy-start(f32[4,45,864]{2,0,1:T(4,128)} %param.17) | copy-start | bytes 1866244
  11.0 21.3 %copy-start.24 = (f32[27]{0:T(128)S(1)}, f32[27]{0:T(128)}, u32[]{:S(2)}) copy-start(f32[27]{0:T(128)} %param.16) | copy-start | bytes 328
  11.0 22.0 %collective-permute-start = (f32[4,2,928]{2,1,0:T(2,128)S(1)}, f32[4,2,928]{2,1,0:T(2,128)S(1)}, u32[]{:S(2)}, u32[]{:S(2)}) collective-permute-start(f32[4,2,928]{2,1,0:T(2,128)S(1)} %get-tuple-element.39), channel_id=1, source_target_pairs={{1,0},{2,1},{3,2},{4,3},{5,4},{6,5},{7,6},{8,7},{9,8},{10,9},{11,1... | collective-permute-start | bytes 89096 | tf_op jit(solution)/shard_map/ppermute | solution.py:25
  25.7 9.2 %collective-permute-start.1 = (f32[4,2,928]{2,1,0:T(2,128)}, f32[4,2,928]{2,1,0:T(2,128)}, u32[]{:S(2)}, u32[]{:S(2)}) collective-permute-start(f32[4,2,928]{2,1,0:T(2,128)} %get-tuple-element.38), channel_id=1, source_target_pairs={{0,1},{1,2},{2,3},{3,4},{4,5},{5,6},{6,7},{7,8},{8,9},{9,10},{10,1... | collective-permute-start | bytes 89096 | tf_op jit(solution)/shard_map/ppermute | solution.py:23
  30.5 10.7 %copy-start.7 = (f32[4,45,32]{2,1,0:T(8,128)}, f32[4,45,32]{2,1,0:T(8,128)S(1)}, u32[]{:S(2)}) copy-start(f32[4,45,32]{2,1,0:T(8,128)S(1)} %copy.57) | copy-start | bytes 69124
  30.6 10.6 %copy-start.9 = (f32[4,45,32]{2,1,0:T(8,128)}, f32[4,45,32]{2,1,0:T(8,128)S(1)}, u32[]{:S(2)}) copy-start(f32[4,45,32]{2,1,0:T(8,128)S(1)} %copy.56) | copy-start | bytes 69124
  33.0 0.6 copy-start.16
  35.8 3.1 copy-start.17
  37.4 2.6 copy-start.2
  39.0 1.1 copy-start.4
  40.0 1.1 copy-start.6
  41.3 4.2 copy-start.23
  41.4 9.9 %copy-start.8 = (f32[4,45,32]{2,1,0:T(8,128)S(1)}, f32[4,45,32]{2,1,0:T(8,128)}, u32[]{:S(2)}) copy-start(f32[4,45,32]{2,1,0:T(8,128)} %copy-done.7) | copy-start | bytes 69124
  41.4 9.9 %copy-start.10 = (f32[4,45,32]{2,1,0:T(8,128)S(1)}, f32[4,45,32]{2,1,0:T(8,128)}, u32[]{:S(2)}) copy-start(f32[4,45,32]{2,1,0:T(8,128)} %copy-done.9) | copy-start | bytes 69124
  42.2 9.1 %collective-permute-start.2 = (f32[2,45,928]{2,1,0:T(8,128)S(1)}, f32[2,45,928]{2,1,0:T(8,128)S(1)}, u32[]{:S(2)}, u32[]{:S(2)}) collective-permute-start(f32[2,45,928]{2,1,0:T(8,128)S(1)} %get-tuple-element.43), channel_id=1, source_target_pairs={{32,0},{64,32},{96,64},{128,96},{160,128},{192,160},{224,192},{256... | collective-permute-start | bytes 1002248 | tf_op jit(solution)/shard_map/ppermute | solution.py:25
  46.1 12.2 %collective-permute-start.3 = (f32[2,45,928]{2,1,0:T(8,128)}, f32[2,45,928]{2,1,0:T(8,128)S(1)}, u32[]{:S(2)}, u32[]{:S(2)}) collective-permute-start(f32[2,45,928]{2,1,0:T(8,128)} %get-tuple-element.42), channel_id=1, source_target_pairs={{0,32},{32,64},{64,96},{96,128},{128,160},{160,192},{192,224},{224... | collective-permute-start | bytes 1002248 | tf_op jit(solution)/shard_map/ppermute | solution.py:23
  58.4 0.7 copy-start.11
  72.7 1.6 copy-start
  72.7 1.6 copy-start.1
  74.8 0.7 copy-start.15
  75.5 1.4 copy-start.22
  75.5 1.4 copy-start.25
  75.5 1.4 copy-start.26
  75.5 274.1 %copy-start.21 = (pred[2]{0:T(512)(128)(4,1)S(1)}, pred[2]{0:T(512)(128)(4,1)}, u32[]{:S(2)}) copy-start(pred[2]{0:T(512)(128)(4,1)} %get-tuple-element.16) | copy-start | bytes 10
  76.9 588.8 %all-reduce.19.cloned.1.call-start = ((), (), s32[]{:S(2)}) async-start(), calls=%async_computation.1 | async-start | bytes 917504 | tf_op jit(solution)/shard_map/psum | solution.py:171
  375.8 289.9 %copy-start.12 = (f32[4,45,864]{2,1,0:T(8,128)S(1)}, f32[4,45,864]{2,1,0:T(8,128)}, u32[]{:S(2)}) copy-start(f32[4,45,864]{2,1,0:T(8,128)} %get-tuple-element.5) | copy-start | bytes 1866244
  668.6 30.9 %copy-start.13 = (f32[4,45,864]{2,1,0:T(8,128)S(1)}, f32[4,45,864]{2,1,0:T(8,128)}, u32[]{:S(2)}) copy-start(f32[4,45,864]{2,1,0:T(8,128)} %get-tuple-element.10) | copy-start | bytes 1866244
  668.6 28.9 %collective-permute-start.4 = (f32[2,45,864]{2,1,0:T(8,128)S(1)}, f32[2,45,864]{2,1,0:T(8,128)S(1)}, u32[]{:S(2)}, u32[]{:S(2)}) collective-permute-start(f32[2,45,864]{2,1,0:T(8,128)S(1)} %slice.204), channel_id=1, source_target_pairs={{0,32},{32,64},{64,96},{96,128},{128,160},{160,192},{192,224},{224... | collective-permute-start | bytes 933128 | tf_op jit(solution)/shard_map/ppermute | solution.py:23
  697.6 9.3 %collective-permute-start.5 = (f32[2,45,864]{2,1,0:T(8,128)S(1)}, f32[2,45,864]{2,1,0:T(8,128)S(1)}, u32[]{:S(2)}, u32[]{:S(2)}) collective-permute-start(f32[2,45,864]{2,1,0:T(8,128)S(1)} %get-tuple-element.27), channel_id=1, source_target_pairs={{32,0},{64,32},{96,64},{128,96},{160,128},{192,160},{224,192},{256... | collective-permute-start | bytes 933128 | tf_op jit(solution)/shard_map/ppermute | solution.py:25
  706.9 0.9 copy-start.3
  706.9 1.0 copy-start.5
  708.8 9.3 %collective-permute-start.6 = (f32[4,2,864]{2,1,0:T(2,128)S(1)}, f32[4,2,864]{2,1,0:T(2,128)S(1)}, u32[]{:S(2)}, u32[]{:S(2)}) collective-permute-start(f32[4,2,864]{2,1,0:T(2,128)S(1)} %get-tuple-element.24), channel_id=1, source_target_pairs={{0,1},{1,2},{2,3},{3,4},{4,5},{5,6},{6,7},{7,8},{8,9},{9,10},{10,1... | collective-permute-start | bytes 82952 | tf_op jit(solution)/shard_map/ppermute | solution.py:23
  710.7 7.9 %collective-permute-start.7 = (f32[4,2,864]{2,1,0:T(2,128)S(1)}, f32[4,2,864]{2,1,0:T(2,128)S(1)}, u32[]{:S(2)}, u32[]{:S(2)}) collective-permute-start(f32[4,2,864]{2,1,0:T(2,128)S(1)} %get-tuple-element.25), channel_id=1, source_target_pairs={{1,0},{2,1},{3,2},{4,3},{5,4},{6,5},{7,6},{8,7},{9,8},{10,9},{11,1... | collective-permute-start | bytes 82952 | tf_op jit(solution)/shard_map/ppermute | solution.py:25
Sparse Core Ops, SparseCore 0:
  77.0 272.5 all-reduce.16
  378.4 287.2 all-reduce.18

commit v2 on v1

--- a/solution.py
+++ b/solution.py
@@ -139,9 +139,10 @@
     )
 
 
-def wave_table(positions, length):
+def wave_table(column_count, length):
+    position = jnp.arange(column_count, dtype=jnp.int32)
     numbers = jnp.arange(KMAX, dtype=jnp.int32)
-    phases = positions[:, None] * numbers[None, :] % length
+    phases = position[:, None] * numbers[None, :] % length
     angles = phases.astype(jnp.float32) * (2.0 * math.pi / length)
     return jnp.concatenate([jnp.cos(angles), jnp.sin(angles)], axis=1)
 
@@ -153,9 +154,17 @@
     return jnp.where(kept_mask, scaling[None, :], 0.0)
 
 
+def lowpass_circles(circles, keep_values):
+    length = circles.shape[2]
+    table_full = wave_table(length, length)
+    coefficient = jnp.einsum("rqn,nk->rqk", circles, table_full, precision=lax.Precision.HIGHEST)
+    coefficient = coefficient * wave_weights(keep_values, length)[:, None, :]
+    lowpass = jnp.einsum("rqk,nk->rqn", coefficient, table_full, precision=lax.Precision.HIGHEST)
+    return jnp.where((keep_values <= KMAX)[:, None, None], lowpass, circles)
+
+
 def filter_field(field, filter_keep):
-    row_count, col_count = field.shape[0], field.shape[1]
-    length = col_count * lax.axis_size("lon")
+    row_count = field.shape[0]
     polar_count = POLAR
     at_north_end = lax.axis_index("lat") == 0
     top_rows = field[:polar_count]
@@ -164,14 +173,11 @@
     end_keep = jnp.where(
         at_north_end, filter_keep[:polar_count], filter_keep[row_count - polar_count :]
     )
-    positions = lax.axis_index("lon") * col_count + jnp.arange(col_count, dtype=jnp.int32)
-    table = wave_table(positions, length)
-    hi = lax.Precision.HIGHEST
-    partial = jnp.einsum("rjq,jk->rkq", end_rows, table, precision=hi)
-    coefficient = lax.psum(partial, "lon")
-    coefficient = coefficient * wave_weights(end_keep, length)[:, :, None]
-    lowpass = jnp.einsum("jk,rkq->rjq", table, coefficient, precision=hi)
-    smoothed = jnp.where((end_keep <= KMAX)[:, None, None], lowpass, end_rows)
+    reordered = jnp.transpose(end_rows, (0, 2, 1))
+    circles = lax.all_to_all(reordered, "lon", split_axis=1, concat_axis=2, tiled=True)
+    lowpass = lowpass_circles(circles, end_keep)
+    smoothed = lax.all_to_all(lowpass, "lon", split_axis=2, concat_axis=1, tiled=True)
+    smoothed = jnp.transpose(smoothed, (0, 2, 1))
     new_top = jnp.where(at_north_end, smoothed, top_rows)
     new_bottom = jnp.where(at_north_end, bottom_rows, smoothed)
     return jnp.concatenate(

time: 729 us -> 291 us (0.40)
  waiting for transfers between devices: 573 us -> 60.3 us
  blocking collectives: 0 us -> 55.4 us
  local copies, waits for them, and re-layouts: 35.5 us -> 72.5 us
  between operations: 14.7 us -> 1.65 us
    psum x2 -> x0, waiting for transfers between devices: 559 us -> none  [filter_field(): coefficient = lax.psum(partial, 'lon')]
    all_to_all x0 -> x2, blocking collectives: none -> 55.4 us  [the longest x1 27.8 us: filter_field(): lax.all_to_all(lowpass, 'lon', split_axis=2, concat_axis=1, tiled=True)]
    all_to_all x0 -> x2, waiting for transfers between devices: none -> 41.6 us  [the longest x1 22.5 us: filter_field(): lax.all_to_all(reordered, 'lon', split_axis=1, concat_axis=2, tiled=True)]
    all_to_all x0 -> x9, local copies, waits for them, and re-layouts: none -> 16 us  [the longest x4 9.65 us: filter_field(): lax.all_to_all(lowpass, 'lon', split_axis=2, concat_axis=1, tiled=True)]
    ppermute x4, starting transfers between devices: 30.9 us -> 16.1 us  [with_halo(): lax.ppermute(tail, axis, [(i, (i + 1) % count) for i in range(ends)])]
    unnamed x61 -> x53, local copies, waits for them, and re-layouts: 8.48 us -> 22.9 us
    all_to_all x0 -> x2, starting transfers between devices: none -> 8.24 us  [the longest x1 4.22 us: filter_field(): lax.all_to_all(lowpass, 'lon', split_axis=2, concat_axis=1, tiled=True)]
  transfers between devices with their start and end apart: 10 -> 10, of which waited for: 6 -> 7; matrix products, arithmetic and copies ran while one was open for 2% -> 6% of each run, Pallas kernels for 0% -> 0%
where the time goes in v2:
time: 291 us; the launch traced here: 286 us
  local copies, waits for them, and re-layouts  72.5 us (25%)
  waiting for transfers between devices  60.3 us (21%)
  blocking collectives  55.4 us (19%)
  starting transfers between devices  51 us (18%)
  Pallas kernels  23.7 us (8%)
  other arithmetic  20 us (7%)
    all_to_all x1, blocking collectives, filter_field(): lax.all_to_all(lowpass, 'lon', split_axis=2, concat_axis=1, tiled=True)  27.8 us
    all_to_all x1, blocking collectives, filter_field(): lax.all_to_all(reordered, 'lon', split_axis=1, concat_axis=2, tiled=True)  27.6 us
    ppermute x4, starting transfers between devices, with_halo(): lax.ppermute(head, axis, [((i + 1) % count, i) for i in range(ends)])  26.7 us
    pallas_call x1, Pallas kernels, chemistry_step(): pl.pallas_call(chem_kernel, grid=(rows,), in_specs=[big, small, big, pl.B...  23.7 us
    unnamed x53, local copies, waits for them, and re-layouts  22.9 us
    all_to_all x1, waiting for transfers between devices, filter_field(): lax.all_to_all(reordered, 'lon', split_axis=1, concat_axis=2, tiled=True)  22.5 us
    all_to_all x1, waiting for transfers between devices, filter_field(): lax.all_to_all(lowpass, 'lon', split_axis=2, concat_axis=1, tiled=True)  19.2 us
    ppermute x4, starting transfers between devices, with_halo(): lax.ppermute(tail, axis, [(i, (i + 1) % count) for i in range(ends)])  16.1 us
  transfers between devices with their start and end apart: 10, of which 7 were waited for; matrix products, arithmetic and copies ran while one was open for 6% of the time, Pallas kernels for 0%

profile of v2, /device:TPU:1, one launch (start us, length us, event | category | flops | bytes accessed | tf_op | source)
XLA Modules:
  0.0 286.5 jit_solution(996105777881944245)
XLA Ops:
  4.5 14.6 %collective-permute-start = (f32[4,2,928]{2,1,0:T(2,128)S(1)}, f32[4,2,928]{2,1,0:T(2,128)S(1)}, u32[]{:S(2)}, u32[]{:S(2)}) collective-permute-start(f32[4,2,928]{2,1,0:T(2,128)S(1)} %get-tuple-element.41), channel_id=1, source_target_pairs={{1,0},{2,1},{3,2},{4,3},{5,4},{6,5},{7,6},{8,7},{9,8},{10,9},{11,1... | collective-permute-start | bytes 89096 | tf_op jit(solution)/shard_map/ppermute | solution.py:25
  19.0 1.9 collective-permute-start.1
  21.8 1.3 copy.110
  23.2 4.4 %collective-permute-done.1 = f32[4,2,928]{2,1,0:T(2,128)} collective-permute-done((f32[4,2,928]{2,1,0:T(2,128)}, f32[4,2,928]{2,1,0:T(2,128)}, u32[]{:S(2)}, u32[]{:S(2)}) %collective-permute-start.1) | collective-permute-done | bytes 29728 | tf_op jit(solution)/shard_map/ppermute | solution.py:23
  28.8 1.2 copy.109
  30.4 1.2 copy.108
  34.9 4.0 %collective-permute-start.2 = (f32[2,45,928]{2,1,0:T(8,128)}, f32[2,45,928]{2,1,0:T(8,128)S(1)}, u32[]{:S(2)}, u32[]{:S(2)}) collective-permute-start(f32[2,45,928]{2,1,0:T(8,128)} %get-tuple-element.45), channel_id=1, source_target_pairs={{32,0},{64,32},{96,64},{128,96},{160,128},{192,160},{224,192},{256... | collective-permute-start | bytes 1002248 | tf_op jit(solution)/shard_map/ppermute | solution.py:25
  38.9 2.7 collective-permute-start.3
  41.6 3.2 %collective-permute-done.2 = f32[2,45,928]{2,1,0:T(8,128)S(1)} collective-permute-done((f32[2,45,928]{2,1,0:T(8,128)}, f32[2,45,928]{2,1,0:T(8,128)S(1)}, u32[]{:S(2)}, u32[]{:S(2)}) %collective-permute-start.2) | collective-permute-done | bytes 334112 | tf_op jit(solution)/shard_map/ppermute | solution.py:25
  45.0 2.4 broadcast_in_dim.96
  47.4 4.5 %reshape.91 = f32[5,45,864]{2,1,0:T(8,128)S(1)} reshape(f32[5,45,32,27]{3,2,1,0:T(8,128)} %broadcast_in_dim.96) | data formatting | bytes 1555200 | tf_op jit(solution)/shard_map/jvp()/reshape | solution.py:33
  52.0 2.8 broadcast_in_dim.97
  54.9 4.3 %eq.87 = pred[5,45,864]{2,1,0:T(8,128)(4,1)S(1)} reshape(pred[5,45,32,27]{3,2,1,0:T(8,128)(4,1)} %broadcast_in_dim.97) | data formatting | bytes 388800 | tf_op jit(solution)/shard_map/jvp()/eq | solution.py:40
  59.1 2.8 broadcast_in_dim.98
  62.0 4.3 %eq.90 = pred[5,45,864]{2,1,0:T(8,128)(4,1)S(1)} reshape(pred[5,45,32,27]{3,2,1,0:T(8,128)(4,1)} %broadcast_in_dim.98) | data formatting | bytes 388800 | tf_op jit(solution)/shard_map/jvp()/eq | solution.py:40
  66.2 1.4 maximum_maximum_fusion
  68.3 1.3 copy.114
  69.5 1.8 reshape.93
  71.4 4.0 %all-to-all-start = ((f32[32,1,2430]{2,1,0:T(1,128)}), f32[32,1,2430]{2,1,0:T(1,128)S(1)}, u32[]{:S(2)}, u32[]{:S(2)}) async-start(f32[32,1,2430]{2,1,0:T(1,128)} %reshape.93), calls=%async_computation | async-start | bytes 622592 | tf_op jit(solution)/shard_map/all_to_all | solution.py:177
  76.4 22.5 %all-to-all-done = f32[32,1,2430]{2,1,0:T(1,128)S(1)} async-done(((f32[32,1,2430]{2,1,0:T(1,128)}), f32[32,1,2430]{2,1,0:T(1,128)S(1)}, u32[]{:S(2)}, u32[]{:S(2)}) %all-to-all-start) | async-done | bytes 311072 | tf_op jit(solution)/shard_map/all_to_all | solution.py:177
  99.4 2.1 reduce
  101.5 1.7 reshape.94
  104.2 1.9 all_to_all.55
  107.0 2.0 copy.119
  109.1 3.7 %reshape.95 = f32[32,1,2430]{2,1,0:T(1,128)} reshape(f32[1440,2,27]{2,1,0:T(2,128)} %bitcast.72) | data formatting | bytes 622080
  112.8 4.2 %all-to-all-start.1 = ((f32[32,1,2430]{2,1,0:T(1,128)}), f32[32,1,2430]{2,1,0:T(1,128)S(1)}, u32[]{:S(2)}, u32[]{:S(2)}) async-start(f32[32,1,2430]{2,1,0:T(1,128)} %reshape.95), calls=%async_computation.1 | async-start | bytes 622592 | tf_op jit(solution)/shard_map/all_to_all | solution.py:179
  117.8 2.0 copy.124.cot_ref
  122.1 19.2 %all-to-all-done.1 = f32[32,1,2430]{2,1,0:T(1,128)S(1)} async-done(((f32[32,1,2430]{2,1,0:T(1,128)}), f32[32,1,2430]{2,1,0:T(1,128)S(1)}, u32[]{:S(2)}, u32[]{:S(2)}) %all-to-all-start.1) | async-done | bytes 311072 | tf_op jit(solution)/shard_map/all_to_all | solution.py:179
  141.3 1.3 reduce.1
  142.6 2.2 reshape.96
  144.8 2.7 copy.166
  147.5 2.8 all_to_all.59
  151.3 23.7 %shard_map.104 = (f32[4,45,864]{2,1,0:T(8,128)}, f32[4,45,864]{2,1,0:T(8,128)}) custom-call(f32[4,45,864]{2,1,0:T(8,128)} %pad_maximum_fusion.3.x_ref, f32[4,45,32]{2,1,0:T(8,128)} %copy.123.seed_ref, f32[4,45,864]{2,1,0:T(8,128)} %copy.124.cot_ref, f32[1,864]{1,0:T(1,128)} %broadcast_in_dim_tile.3.sat_ref, f32[32,864]{1,0:T(8,128)} %fusion.21.spread_ref, ...), custom_call_target="tpu_custom_call" | custom-call | tf_op jit(solution)/shard_map/pallas_call | solution.py:242
  178.3 27.6 %all_to_all.72 = f32[32,1,2430]{2,1,0:T(1,128)S(1)} all-to-all(f32[32,1,2430]{2,1,0:T(1,128)S(1)} %reshape.97), channel_id=1, replica_groups=mesh['lat'=16,'lon'=32] {'lon'}, dimensions={0} | all-to-all | bytes 622080 | tf_op jit(solution)/shard_map/all_to_all | solution.py:177
  205.9 1.3 reduce.2
  208.9 1.9 all_to_all.63
  211.8 1.5 copy.130
  213.3 1.6 reshape.99
  215.0 27.8 %all_to_all.73 = f32[32,1,2430]{2,1,0:T(1,128)S(1)} all-to-all(f32[32,1,2430]{2,1,0:T(1,128)S(1)} %reshape.99), channel_id=1, replica_groups=mesh['lat'=16,'lon'=32] {'lon'}, dimensions={0} | all-to-all | bytes 622080 | tf_op jit(solution)/shard_map/all_to_all | solution.py:179
  242.7 1.3 reduce.3
  245.1 1.4 copy.165
  246.5 2.8 all_to_all.67
  251.6 8.8 %collective-permute-start.4 = (f32[2,45,864]{2,1,0:T(8,128)S(1)}, f32[2,45,864]{2,1,0:T(8,128)S(1)}, u32[]{:S(2)}, u32[]{:S(2)}) collective-permute-start(f32[2,45,864]{2,1,0:T(8,128)S(1)} %slice.204), channel_id=1, source_target_pairs={{0,32},{32,64},{64,96},{96,128},{128,160},{160,192},{192,224},{224... | collective-permute-start | bytes 933128 | tf_op jit(solution)/shard_map/ppermute | solution.py:23
  260.4 4.2 %collective-permute-done.4 = f32[2,45,864]{2,1,0:T(8,128)S(1)} collective-permute-done((f32[2,45,864]{2,1,0:T(8,128)S(1)}, f32[2,45,864]{2,1,0:T(8,128)S(1)}, u32[]{:S(2)}, u32[]{:S(2)}) %collective-permute-start.4) | collective-permute-done | bytes 311072 | tf_op jit(solution)/shard_map/ppermute | solution.py:23
  264.7 1.9 collective-permute-start.5
  267.7 6.3 %collective-permute-done.5 = f32[2,45,864]{2,1,0:T(8,128)S(1)} collective-permute-done((f32[2,45,864]{2,1,0:T(8,128)S(1)}, f32[2,45,864]{2,1,0:T(8,128)S(1)}, u32[]{:S(2)}, u32[]{:S(2)}) %collective-permute-start.5) | collective-permute-done | bytes 311072 | tf_op jit(solution)/shard_map/ppermute | solution.py:25
  275.0 2.7 collective-permute-start.6
  277.8 6.2 %collective-permute-start.7 = (f32[4,2,864]{2,1,0:T(2,128)S(1)}, f32[4,2,864]{2,1,0:T(2,128)S(1)}, u32[]{:S(2)}, u32[]{:S(2)}) collective-permute-start(f32[4,2,864]{2,1,0:T(2,128)S(1)} %get-tuple-element.27), channel_id=1, source_target_pairs={{1,0},{2,1},{3,2},{4,3},{5,4},{6,5},{7,6},{8,7},{9,8},{10,9},{11,1... | collective-permute-start | bytes 82952 | tf_op jit(solution)/shard_map/ppermute | solution.py:25
  (114 shorter events, 31.6 us)
Async XLA Ops:
  0.6 20.3 %copy-start.14 = (s32[4,45,32]{1,2,0:T(8,128)S(1)}, s32[4,45,32]{1,2,0:T(8,128)}, u32[]{:S(2)}) copy-start(s32[4,45,32]{1,2,0:T(8,128)} %param.13) | copy-start | bytes 69124
  1.6 19.5 %copy-start.15 = (f32[4,45,32]{1,2,0:T(8,128)S(1)}, f32[4,45,32]{1,2,0:T(8,128)}, u32[]{:S(2)}) copy-start(f32[4,45,32]{1,2,0:T(8,128)} %param.11) | copy-start | bytes 69124
  4.5 16.8 %collective-permute-start = (f32[4,2,928]{2,1,0:T(2,128)S(1)}, f32[4,2,928]{2,1,0:T(2,128)S(1)}, u32[]{:S(2)}, u32[]{:S(2)}) collective-permute-start(f32[4,2,928]{2,1,0:T(2,128)S(1)} %get-tuple-element.41), channel_id=1, source_target_pairs={{1,0},{2,1},{3,2},{4,3},{5,4},{6,5},{7,6},{8,7},{9,8},{10,9},{11,1... | collective-permute-start | bytes 89096 | tf_op jit(solution)/shard_map/ppermute | solution.py:25
  19.0 8.6 %collective-permute-start.1 = (f32[4,2,928]{2,1,0:T(2,128)}, f32[4,2,928]{2,1,0:T(2,128)}, u32[]{:S(2)}, u32[]{:S(2)}) collective-permute-start(f32[4,2,928]{2,1,0:T(2,128)} %get-tuple-element.40), channel_id=1, source_target_pairs={{0,1},{1,2},{2,3},{3,4},{4,5},{5,6},{6,7},{7,8},{8,9},{9,10},{10,1... | collective-permute-start | bytes 89096 | tf_op jit(solution)/shard_map/ppermute | solution.py:23
  21.2 0.6 copy-start.12
  28.4 3.1 %copy-start.13 = (f32[4,2,928]{2,1,0:T(2,128)S(1)}, f32[4,2,928]{2,1,0:T(2,128)}, u32[]{:S(2)}) copy-start(f32[4,2,928]{2,1,0:T(2,128)} %copy-done.12) | copy-start | bytes 89092
  30.0 2.6 copy-start.5
  31.6 1.5 copy-start.7
  32.6 1.1 copy-start.9
  34.9 9.9 %collective-permute-start.2 = (f32[2,45,928]{2,1,0:T(8,128)}, f32[2,45,928]{2,1,0:T(8,128)S(1)}, u32[]{:S(2)}, u32[]{:S(2)}) collective-permute-start(f32[2,45,928]{2,1,0:T(8,128)} %get-tuple-element.45), channel_id=1, source_target_pairs={{32,0},{64,32},{96,64},{128,96},{160,128},{192,160},{224,192},{256... | collective-permute-start | bytes 1002248 | tf_op jit(solution)/shard_map/ppermute | solution.py:25
  38.9 13.0 %collective-permute-start.3 = (f32[2,45,928]{2,1,0:T(8,128)}, f32[2,45,928]{2,1,0:T(8,128)S(1)}, u32[]{:S(2)}, u32[]{:S(2)}) collective-permute-start(f32[2,45,928]{2,1,0:T(8,128)} %get-tuple-element.44), channel_id=1, source_target_pairs={{0,32},{32,64},{64,96},{96,128},{128,160},{160,192},{192,224},{224... | collective-permute-start | bytes 1002248 | tf_op jit(solution)/shard_map/ppermute | solution.py:23
  51.9 3.0 %copy-start.10 = (f32[2,45,928]{2,1,0:T(8,128)}, f32[2,45,928]{2,1,0:T(8,128)S(1)}, u32[]{:S(2)}) copy-start(f32[2,45,928]{2,1,0:T(8,128)S(1)} %collective-permute-done.3) | copy-start | bytes 1002244
  59.1 8.5 %copy-start = (pred[5,45,864]{2,1,0:T(8,128)(4,1)}, pred[5,45,864]{2,1,0:T(8,128)(4,1)S(1)}, u32[]{:S(2)}) copy-start(pred[5,45,864]{2,1,0:T(8,128)(4,1)S(1)} %eq.87) | copy-start | bytes 583204
  66.2 1.4 copy-start.2
  68.2 7.2 %copy-start.17 = (s32[4]{0:T(128)S(1)}, s32[4]{0:T(128)}, u32[]{:S(2)}) copy-start(s32[4]{0:T(128)} %param.14) | copy-start | bytes 52
  71.4 27.5 %all-to-all-start = ((f32[32,1,2430]{2,1,0:T(1,128)}), f32[32,1,2430]{2,1,0:T(1,128)S(1)}, u32[]{:S(2)}, u32[]{:S(2)}) async-start(f32[32,1,2430]{2,1,0:T(1,128)} %reshape.93), calls=%async_computation | async-start | bytes 622592 | tf_op jit(solution)/shard_map/all_to_all | solution.py:177
  109.1 8.0 %copy-start.16 = (f32[4,45,32]{1,2,0:T(8,128)S(1)}, f32[4,45,32]{1,2,0:T(8,128)}, u32[]{:S(2)}) copy-start(f32[4,45,32]{1,2,0:T(8,128)} %param.15) | copy-start | bytes 69124
  112.8 7.0 %copy-start.18 = (f32[27]{0:T(128)S(1)}, f32[27]{0:T(128)}, u32[]{:S(2)}) copy-start(f32[27]{0:T(128)} %param.16) | copy-start | bytes 328
  112.8 28.5 %all-to-all-start.1 = ((f32[32,1,2430]{2,1,0:T(1,128)}), f32[32,1,2430]{2,1,0:T(1,128)S(1)}, u32[]{:S(2)}, u32[]{:S(2)}) async-start(f32[32,1,2430]{2,1,0:T(1,128)} %reshape.95), calls=%async_computation.1 | async-start | bytes 622592 | tf_op jit(solution)/shard_map/all_to_all | solution.py:179
  246.5 2.8 copy-start.4
  249.4 0.9 copy-start.1
  249.4 1.0 copy-start.3
  251.6 15.0 %copy-start.11 = (f32[4,45,864]{2,1,0:T(8,128)S(1)}, f32[4,45,864]{2,1,0:T(8,128)}, u32[]{:S(2)}) copy-start(f32[4,45,864]{2,1,0:T(8,128)} %get-tuple-element.12) | copy-start | bytes 1866244
  251.6 13.0 %collective-permute-start.4 = (f32[2,45,864]{2,1,0:T(8,128)S(1)}, f32[2,45,864]{2,1,0:T(8,128)S(1)}, u32[]{:S(2)}, u32[]{:S(2)}) collective-permute-start(f32[2,45,864]{2,1,0:T(8,128)S(1)} %slice.204), channel_id=1, source_target_pairs={{0,32},{32,64},{64,96},{96,128},{128,160},{160,192},{192,224},{224... | collective-permute-start | bytes 933128 | tf_op jit(solution)/shard_map/ppermute | solution.py:23
  264.7 9.3 %collective-permute-start.5 = (f32[2,45,864]{2,1,0:T(8,128)S(1)}, f32[2,45,864]{2,1,0:T(8,128)S(1)}, u32[]{:S(2)}, u32[]{:S(2)}) collective-permute-start(f32[2,45,864]{2,1,0:T(8,128)S(1)} %get-tuple-element.29), channel_id=1, source_target_pairs={{32,0},{64,32},{96,64},{128,96},{160,128},{192,160},{224,192},{256... | collective-permute-start | bytes 933128 | tf_op jit(solution)/shard_map/ppermute | solution.py:25
  267.7 6.4 %copy-start.6 = (pred[4,46,864]{2,1,0:T(8,128)(4,1)S(1)}, pred[4,46,864]{2,1,0:T(8,128)(4,1)}, u32[]{:S(2)}) copy-start(pred[4,46,864]{2,1,0:T(8,128)(4,1)} %copy-done.5) | copy-start | bytes 476932
  267.7 6.4 %copy-start.8 = (pred[4,46,864]{2,1,0:T(8,128)(4,1)S(1)}, pred[4,46,864]{2,1,0:T(8,128)(4,1)}, u32[]{:S(2)}) copy-start(pred[4,46,864]{2,1,0:T(8,128)(4,1)} %copy-done.7) | copy-start | bytes 476932
  275.0 9.3 %collective-permute-start.6 = (f32[4,2,864]{2,1,0:T(2,128)S(1)}, f32[4,2,864]{2,1,0:T(2,128)S(1)}, u32[]{:S(2)}, u32[]{:S(2)}) collective-permute-start(f32[4,2,864]{2,1,0:T(2,128)S(1)} %get-tuple-element.26), channel_id=1, source_target_pairs={{0,1},{1,2},{2,3},{3,4},{4,5},{5,6},{6,7},{7,8},{8,9},{9,10},{10,1... | collective-permute-start | bytes 82952 | tf_op jit(solution)/shard_map/ppermute | solution.py:23
  277.8 7.1 %collective-permute-start.7 = (f32[4,2,864]{2,1,0:T(2,128)S(1)}, f32[4,2,864]{2,1,0:T(2,128)S(1)}, u32[]{:S(2)}, u32[]{:S(2)}) collective-permute-start(f32[4,2,864]{2,1,0:T(2,128)S(1)} %get-tuple-element.27), channel_id=1, source_target_pairs={{1,0},{2,1},{3,2},{4,3},{5,4},{6,5},{7,6},{8,7},{9,8},{10,9},{11,1... | collective-permute-start | bytes 82952 | tf_op jit(solution)/shard_map/ppermute | solution.py:25
